TPU v7x, 512 devices: a whole 4x4x16 slice. The times are simulated.
512 devices in a mesh: dp: 2 (over z_hi), fsdp: 16 (over z_lo, core), tile: 16 (over y, x).
Axes of the slice: x: 4, y: 4, z: 16 (z_hi: 2, z_lo: 8; z = z_hi * 8 + z_lo), core: 2. Of those that a mesh axis runs over, the one named last changes fastest.
Arguments:
- tokens: bfloat16 [32, 8, 512, 1536], P(('dp', 'fsdp'), None, 'tile'), may hold values from -6 to 6
- norm_gain: float32 [1536], replicated, may hold values from 0.25 to 1.75
- query_key_value_weight: bfloat16 [1536, 2304], P('fsdp'), may hold values from -5 to 5
- out_weight: bfloat16 [768, 1536], P('fsdp'), may hold values from -0.21875 to 0.21875
- head_weight: bfloat16 [1536, 320], P('fsdp'), may hold values from -0.15625 to 0.15625
- coarse: float32 [32, 20, 8, 512], P(('dp', 'fsdp'), None, None, 'tile'), may hold values from -36 to 36
- grad_fine: float32 [32, 20, 32, 2048], P(('dp', 'fsdp'), None, None, 'tile'), may hold values from -0.6 to 0.6
Outputs:
- fine_grid: float32 [32, 20, 32, 2048], P(('dp', 'fsdp'), None, None, 'tile')
- grad_tokens: bfloat16 [32, 8, 512, 1536], P(('dp', 'fsdp'), None, 'tile')
- grad_head: float32 [1536, 320], P('fsdp')
All inputs are finite; a program needn't handle non-finite values.
Results may differ from a plain program's by a relative error of at most 0.0059.
Values may be sent and summed in bfloat16 or wider, within the bound.
No kernel may reach another device: no remote copies, remote signals or barrier semaphores. Data moves between devices by JAX's collectives and lax.ppermute only.
A program may use at most 64 MiB of HBM per device.

v0:
```python
import jax
import jax.numpy as jnp
from jax import lax
from jax.sharding import Mesh
from jax.sharding import PartitionSpec as P

D = 1536
HEADS = 8
HEAD_DIM = 96
VARS = 20
MARGIN = 8
INNER = 768
HEAD_OUT = 320
EPSILON = 1e-05


def with_halo(shard, sides, width):
    for axis, dim in sides:
        devices, length = (lax.axis_size(axis), shard.shape[dim])
        up = [(i, (i + 1) % devices) for i in range(devices)]
        down = [(j, i) for i, j in up]
        last = lax.slice_in_dim(shard, length - width, length, axis=dim)
        leading = lax.slice_in_dim(shard, 0, width, axis=dim)
        before = lax.ppermute(last, axis, up)
        after = lax.ppermute(leading, axis, down)
        shard = jnp.concatenate([before, shard, after], axis=dim)
    return shard


def from_behind(value, axis, steps):
    count = lax.axis_size(axis)
    pairs = [(source, (source + steps) % count) for source in range(count)]
    return lax.ppermute(value, axis, pairs)


def layer_norm(values):
    average = jnp.mean(values, axis=-1, keepdims=True)
    centred = values - average
    variance = jnp.mean(centred * centred, axis=-1, keepdims=True)
    inverse_dev = lax.rsqrt(variance + EPSILON)
    return (centred * inverse_dev, inverse_dev)


def norm_backward(grad_normed, standard, inverse_dev, norm_gain):
    grad_standard = grad_normed * norm_gain
    first_mean = jnp.mean(grad_standard, axis=-1, keepdims=True)
    second_mean = jnp.mean(grad_standard * standard, axis=-1, keepdims=True)
    return inverse_dev * (grad_standard - first_mean - standard * second_mean)


def attend_forward(queries, keys_values):
    query_count = queries.shape[0]
    key_count = keys_values.shape[0]
    score_scale = HEAD_DIM ** (-0.5)
    query_heads = queries.reshape(query_count, HEADS, HEAD_DIM)
    key_heads = keys_values[:, :INNER].reshape(key_count, HEADS, HEAD_DIM)
    value_heads = keys_values[:, INNER:].reshape(key_count, HEADS, HEAD_DIM)
    scores = (
        jnp.einsum("qhd,khd->hqk", query_heads, key_heads, preferred_element_type=jnp.float32)
        * score_scale
    )
    biggest = jnp.max(scores, axis=-1, keepdims=True)
    exponent = jnp.exp(scores - biggest)
    softmax_out = exponent / jnp.sum(exponent, axis=-1, keepdims=True)
    softmax_low = softmax_out.astype(jnp.bfloat16)
    attended = jnp.einsum(
        "hqk,khd->qhd", softmax_low, value_heads, preferred_element_type=jnp.float32
    )
    return (attended.astype(jnp.bfloat16).reshape(query_count, INNER), softmax_out)


def attend_backward(softmax_out, queries, keys_values, grad_attended):
    query_count = queries.shape[0]
    key_count = keys_values.shape[0]
    score_scale = HEAD_DIM ** (-0.5)
    query_heads = queries.reshape(query_count, HEADS, HEAD_DIM)
    key_heads = keys_values[:, :INNER].reshape(key_count, HEADS, HEAD_DIM)
    value_heads = keys_values[:, INNER:].reshape(key_count, HEADS, HEAD_DIM)
    grad_heads = grad_attended.reshape(query_count, HEADS, HEAD_DIM)
    softmax_low = softmax_out.astype(jnp.bfloat16)
    grad_values = jnp.einsum(
        "hqk,qhd->khd", softmax_low, grad_heads, preferred_element_type=jnp.float32
    )
    grad_weights = jnp.einsum(
        "qhd,khd->hqk", grad_heads, value_heads, preferred_element_type=jnp.float32
    )
    weighted = jnp.sum(softmax_out * grad_weights, axis=-1, keepdims=True)
    grad_scores = (softmax_out * (grad_weights - weighted)).astype(jnp.bfloat16)
    grad_queries = (
        jnp.einsum("hqk,khd->qhd", grad_scores, key_heads, preferred_element_type=jnp.float32)
        * score_scale
    )
    grad_keys = (
        jnp.einsum("hqk,qhd->khd", grad_scores, query_heads, preferred_element_type=jnp.float32)
        * score_scale
    )
    pair_gradient_rows = jnp.concatenate(
        [grad_keys.reshape(key_count, INNER), grad_values.reshape(key_count, INNER)], axis=1
    )
    return (grad_queries.astype(jnp.bfloat16).reshape(query_count, INNER), pair_gradient_rows)


def interp_weights(fine_index):
    coarse_cell = fine_index // 4
    phase_index = fine_index % 4
    lower_shift = (phase_index < 2).astype(jnp.int32)
    upper_weight = (2 * phase_index - 3 + 8 * lower_shift).astype(jnp.float32) / 8.0
    return (coarse_cell - lower_shift, upper_weight)


def build_matrix(lower_cell, upper_cell, upper_weight, count):
    columns = jnp.arange(count, dtype=jnp.int32)
    lower_part = jnp.where(
        columns[None, :] == lower_cell[:, None], 1.0 - upper_weight[:, None], 0.0
    )
    upper_portion = jnp.where(columns[None, :] == upper_cell[:, None], upper_weight[:, None], 0.0)
    return lower_part + upper_portion


def contract_last(left_side, right_side):
    return lax.dot_general(
        left_side, right_side, (((1,), (1,)), ((), ())), preferred_element_type=jnp.float32
    )


ZS = 8
CORES = 2
YS = 4
XS = 4
FSDP = ("z", "c")
TILE = ("y", "x")
HALF_QKV = 1152
HALF_OUT = 768


def gather_weights(qkv, out_w, head_w):
    half = lax.axis_index("dp")
    qkv_half = lax.dynamic_slice_in_dim(qkv, half * HALF_QKV, HALF_QKV, 1)
    out_half = lax.dynamic_slice_in_dim(out_w, half * HALF_OUT, HALF_OUT, 1)
    out_half = jnp.concatenate([out_half[:, :384], out_half[:, 384:]], axis=0)
    head_half = lax.dynamic_slice_in_dim(head_w, half * 160, 160, 1)
    packed = jnp.concatenate([qkv_half, out_half, head_half], axis=1)
    full = lax.all_gather(packed, ("dp",) + FSDP, axis=0, tiled=True)
    full = full.reshape(2, D, 1696)
    full_qkv = jnp.concatenate([full[0, :, :HALF_QKV], full[1, :, :HALF_QKV]], axis=1)
    out_part = full[:, :, HALF_QKV:1536].reshape(2, 16, 2, 48, 384)
    full_out = out_part.transpose(1, 3, 0, 2, 4).reshape(INNER, D)
    full_head = jnp.concatenate([full[0, :, 1536:], full[1, :, 1536:]], axis=1)
    return (full_qkv, full_out, full_head)


def reduce_head(head_term):
    core = lax.axis_index("c")
    parts = head_term.reshape(ZS, CORES, 96, HEAD_OUT)
    own = lax.dynamic_index_in_dim(parts, core, 1, keepdims=False)
    other = lax.dynamic_index_in_dim(parts, 1 - core, 1, keepdims=False)
    pair = own + lax.ppermute(other, "c", [(0, 1), (1, 0)])
    pieces = pair.reshape(ZS, 16, 6, HEAD_OUT).transpose(1, 0, 2, 3).astype(jnp.bfloat16)
    pieces = lax.all_to_all(pieces, TILE, 0, 0, tiled=True)
    over_tile = jnp.sum(pieces.astype(jnp.float32), axis=0)
    both = jnp.broadcast_to(over_tile[None], (2, ZS, 6, HEAD_OUT)).reshape(2 * ZS, 6, HEAD_OUT)
    both = lax.all_to_all(both, ("dp", "z"), 0, 0, tiled=True)
    total = jnp.sum(both, axis=0)
    spread = jnp.broadcast_to(total[None], (16, 6, HEAD_OUT))
    return lax.all_to_all(spread, TILE, 0, 0, tiled=True).reshape(96, HEAD_OUT)


def shards(tokens, norm_gain, query_key_value_weight, out_weight, head_weight, coarse, grad_fine):
    lat_rows = tokens.shape[1]
    lon_cols = tokens.shape[2]
    row_count = lat_rows * lon_cols
    flattened_rows = tokens[0].reshape(row_count, D).astype(jnp.float32)
    standard, inverse_dev = layer_norm(flattened_rows)
    normed = (standard * norm_gain).astype(jnp.bfloat16)
    full_qkv, full_out, full_head = gather_weights(query_key_value_weight, out_weight, head_weight)
    projected = jnp.dot(normed, full_qkv, preferred_element_type=jnp.float32).astype(jnp.bfloat16)
    queries = projected[:, :INNER]
    pairs_local = projected[:, INNER:]
    margin_pairs = with_halo(
        pairs_local.reshape(lat_rows, lon_cols, 2 * INNER), ((TILE, 1),), MARGIN
    )
    keys_values = margin_pairs.reshape(lat_rows * (lon_cols + 2 * MARGIN), 2 * INNER)
    attended, softmax_out = attend_forward(queries, keys_values)
    mixed_out = jnp.dot(attended, full_out, preferred_element_type=jnp.float32)
    hidden = (flattened_rows + mixed_out).astype(jnp.bfloat16)
    head_out = jnp.dot(hidden, full_head, preferred_element_type=jnp.float32)
    fine_head = (
        head_out.reshape(lat_rows, lon_cols, VARS, 4, 4)
        .transpose(2, 0, 3, 1, 4)
        .reshape(VARS, 4 * lat_rows, 4 * lon_cols)
    )
    coarse_padded_grid = with_halo(coarse[0], ((TILE, 2),), 1)
    lat_lower, lat_upper_weight = interp_weights(jnp.arange(4 * lat_rows, dtype=jnp.int32))
    latitude_matrix = build_matrix(
        jnp.clip(lat_lower, 0, lat_rows - 1),
        jnp.clip(lat_lower + 1, 0, lat_rows - 1),
        lat_upper_weight,
        lat_rows,
    )
    lon_lower, lon_upper_weight = interp_weights(jnp.arange(4 * lon_cols, dtype=jnp.int32))
    lon_matrix = build_matrix(lon_lower + 1, lon_lower + 2, lon_upper_weight, lon_cols + 2)
    incomplete_grid = jnp.einsum(
        "lj,kji->kli", latitude_matrix, coarse_padded_grid, precision=lax.Precision.HIGHEST
    )
    residual = jnp.einsum(
        "vrb,cb->vrc", incomplete_grid, lon_matrix, precision=lax.Precision.HIGHEST
    )
    fine_grid = fine_head + residual
    grad_rows = (
        grad_fine[0]
        .reshape(VARS, lat_rows, 4, lon_cols, 4)
        .transpose(1, 3, 0, 2, 4)
        .reshape(row_count, HEAD_OUT)
    )
    grad_rows = grad_rows.astype(jnp.bfloat16)
    head_term = lax.dot_general(
        hidden, grad_rows, (((0,), (0,)), ((), ())), preferred_element_type=jnp.float32
    )
    grad_head = reduce_head(head_term)
    grad_hidden = contract_last(grad_rows, full_head)
    grad_attended = contract_last(grad_hidden.astype(jnp.bfloat16), full_out).astype(jnp.bfloat16)
    grad_queries, pair_gradient_rows = attend_backward(
        softmax_out, queries, keys_values, grad_attended
    )
    pair_gradient_rows = pair_gradient_rows.reshape(lat_rows, lon_cols + 2 * MARGIN, 2 * INNER)
    from_left = from_behind(pair_gradient_rows[:, lon_cols + MARGIN :], TILE, 1)
    from_right = from_behind(pair_gradient_rows[:, :MARGIN], TILE, -1)
    own_cells = pair_gradient_rows[:, MARGIN : MARGIN + lon_cols]
    own_cells = own_cells + jnp.pad(from_left, ((0, 0), (0, lon_cols - MARGIN), (0, 0)))
    own_cells = own_cells + jnp.pad(from_right, ((0, 0), (lon_cols - MARGIN, 0), (0, 0)))
    grad_all = jnp.concatenate(
        [grad_queries, own_cells.reshape(row_count, 2 * INNER).astype(jnp.bfloat16)], axis=1
    )
    grad_normed = contract_last(grad_all, full_qkv)
    grad_input = grad_hidden + norm_backward(grad_normed, standard, inverse_dev, norm_gain)
    grad_tokens = grad_input.astype(jnp.bfloat16).reshape(1, lat_rows, lon_cols, D)
    return (fine_grid[None], grad_tokens, grad_head)


def solution(mesh):
    fine_mesh = Mesh(mesh.devices.reshape(2, ZS, CORES, YS, XS), ("dp", "z", "c", "y", "x"))
    samples = ("dp", "z", "c")
    placed = (
        P(samples, None, TILE, None),
        P(),
        P(FSDP, None),
        P(FSDP, None),
        P(FSDP, None),
        P(samples, None, None, TILE),
        P(samples, None, None, TILE),
    )
    return jax.shard_map(
        shards,
        mesh=fine_mesh,
        in_specs=placed,
        out_specs=(P(samples, None, None, TILE), P(samples, None, TILE, None), P(FSDP, None)),
        check_vma=False,
    )
```

profile of v0, /device:TPU:32, one launch (start us, length us, event | category | flops | bytes accessed | tf_op | source)
XLA Modules:
  0.0 268.6 jit_solution(15269680158934245788)
XLA Ops:
  10.0 3.4 %collective-permute-start.2 = (f32[20,8,1]{2,1,0:T(8,128)S(1)}, f32[20,8,1]{2,1,0:T(8,128)S(1)}, u32[]{:S(2)}, u32[]{:S(2)}) collective-permute-start(f32[20,8,1]{2,1,0:T(8,128)S(1)} %get-tuple-element.17), channel_id=1, source_target_pairs={{0,1},{1,2},{2,3},{3,4},{4,5},{5,6},{6,7},{7,8},{8,9},{9,10},{10,1... | collective-permute-start | bytes 1928 | tf_op jit(solution)/shard_map/ppermute | solution.py:24
  13.4 5.8 %collective-permute-start.3 = (f32[20,8,1]{2,1,0:T(8,128)S(1)}, f32[20,8,1]{2,1,0:T(8,128)S(1)}, u32[]{:S(2)}, u32[]{:S(2)}) collective-permute-start(f32[20,8,1]{2,1,0:T(8,128)S(1)} %get-tuple-element.18), channel_id=1, source_target_pairs={{1,0},{2,1},{3,2},{4,3},{5,4},{6,5},{7,6},{8,7},{9,8},{10,9},{11,1... | collective-permute-start | bytes 1928 | tf_op jit(solution)/shard_map/ppermute | solution.py:25
  19.8 1.5 copy.80
  27.0 70.3 %all-gather.2.cloned.1.call-done = bf16[3072,1696]{1,0:T(8,128)(2,1)} async-done(((bf16[96,1696]{1,0:T(8,128)(2,1)}), bf16[3072,1696]{1,0:T(8,128)(2,1)}) %all-gather.2.cloned.1.call-update) | async-done | bytes 10420240 | tf_op jit(solution)/shard_map/all_gather | solution.py:143
  97.3 2.6 slice_bitcast_fusion.3
  100.0 1.9 slice.82
  101.9 3.7 %slice_bitcast_fusion.1 = (bf16[1536,1152]{1,0:T(8,128)(2,1)S(1)}, bf16[1536,1152]{1,0:T(8,128)(2,1)S(1)}) fusion(bf16[2,1536,1696]{2,1,0:T(8,128)(2,1)} %bitcast.108), kind=kLoop, calls=%fused_computation.6 | loop fusion | bytes 14155776 | tf_op jit(solution)/shard_map/squeeze | solution.py:145
  105.6 3.8 %fusion.3 = bf16[256,2304]{1,0:T(8,128)(2,1)S(1)} fusion(bf16[256,1536]{1,0:T(8,128)(2,1)S(1)} %multiply_convert_fusion.1, bf16[1536,1152]{1,0:T(8,128)(2,1)S(1)} %get-tuple-element.8, bf16[1536,1152]{1,0:T(8,128)(2,1)S(1)} %get-tuple-element.7), kind=kOutput, calls=%fused_computation.4 | convolution fusion | flops 1826684928 | bytes 9043968 | tf_op jit(solution)/shard_map/dot_general | solution.py:176
  111.1 3.7 %copy.76 = bf16[16,48,2,2,384]{4,3,2,1,0:T(2,128)(2,1)} copy(bf16[16,48,2,2,384]{4,1,3,0,2:T(8,128)(2,1)S(1)} %bitcast.109) | data formatting | bytes 4718592 | tf_op jit(solution)/shard_map/transpose | solution.py:147
  114.8 5.3 %reshape.212 = bf16[768,1536]{1,0:T(8,128)(2,1)S(1)} reshape(bf16[16,48,2,2,384]{4,3,2,1,0:T(2,128)(2,1)} %copy.76) | data formatting | bytes 4718592 | tf_op jit(solution)/shard_map/reshape | solution.py:147
  121.3 1.8 fusion.66
  123.1 3.4 %collective-permute-start = (bf16[8,8,1536]{2,1,0:T(8,128)(2,1)}, bf16[8,8,1536]{2,1,0:T(8,128)(2,1)}, u32[]{:S(2)}, u32[]{:S(2)}) collective-permute-start(bf16[8,8,1536]{2,1,0:T(8,128)(2,1)} %get-tuple-element.13), channel_id=1, source_target_pairs={{0,1},{1,2},{2,3},{3,4},{4,5},{5,6},{6,7},{7,8},{8,9},{9,10},{10,1... | collective-permute-start | bytes 589832 | tf_op jit(solution)/shard_map/ppermute | solution.py:24
  126.4 6.0 %collective-permute-start.1 = (bf16[8,8,1536]{2,1,0:T(8,128)(2,1)}, bf16[8,8,1536]{2,1,0:T(8,128)(2,1)}, u32[]{:S(2)}, u32[]{:S(2)}) collective-permute-start(bf16[8,8,1536]{2,1,0:T(8,128)(2,1)} %get-tuple-element.14), channel_id=1, source_target_pairs={{1,0},{2,1},{3,2},{4,3},{5,4},{6,5},{7,6},{8,7},{9,8},{10,9},{11,1... | collective-permute-start | bytes 589832 | tf_op jit(solution)/shard_map/ppermute | solution.py:25
  132.4 2.1 convolution_bitcast_fusion
  135.6 1.6 convolution_convert_fusion
  137.2 1.9 copy.81
  141.6 2.1 copy.92
  143.8 2.1 copy.91
  145.9 3.9 %fusion.68 = (f32[8,256]{1,0:T(8,128)S(1)}, f32[8,256,384]{2,1,0:T(8,128)}) fusion(bf16[256,8,96]{0,2,1:T(8,128)(2,1)S(1)} %bitcast.117, bf16[384,8,96]{0,2,1:T(8,128)(2,1)} %bitcast.111), kind=kOutput, calls=%fused_computation.133 | convolution fusion | flops 153354624 | bytes 4136960 | tf_op jit(solution)/shard_map/sub | solution.py:63
  149.8 2.9 %convolution_convert_fusion.1 = bf16[8,96,256]{2,1,0:T(8,128)(2,1)S(1)} fusion(bf16[384,8,96]{0,2,1:T(8,128)(2,1)} %bitcast.127, f32[8,256,384]{2,1,0:T(8,128)} %get-tuple-element.20, f32[8,256]{1,0:T(8,128)S(1)} %get-tuple-element.19), kind=kOutput, calls=%fused_computation.33 | convolution fusion | flops 152764416 | bytes 4136960 | tf_op jit(solution)/shard_map/hqk,khd->qhd/dot_general | solution.py:66
  152.9 1.6 convolution_bitcast_fusion.1
  156.6 1.4 fusion.14
  158.0 1.4 fusion.13
  159.4 1.7 fusion.8
  161.1 2.4 copy.85
  163.4 1.7 fusion.26
  166.3 1.9 collective-permute-start.6
  169.2 1.4 reshape.213
  170.7 3.1 %copy.77 = f32[8,32,20,4,4]{2,4,1,3,0:T(4,128)} copy(f32[8,32,20,4,4]{1,0,4,3,2:T(8,128)} %reshape.213) | data formatting | bytes 655360 | tf_op jit(solution)/shard_map/reshape | solution.py:188
  173.7 3.0 %copy.78 = f32[20,32,128]{2,1,0:T(8,128)} copy(f32[20,32,128]{0,2,1:T(8,128)} %bitcast.110) | data formatting | bytes 655360 | tf_op jit(solution)/shard_map/reshape | solution.py:190
  176.7 3.0 %copy.83 = f32[384,8,96]{2,1,0:T(8,128)} copy(f32[384,8,96]{0,2,1:T(8,128)} %convolution_bitcast_fusion.1) | data formatting | bytes 2359296 | tf_op jit(solution)/shard_map/hqk,qhd->khd/transpose | solution.py:81
  179.7 2.8 %concatenate.36 = f32[8,48,768]{2,1,0:T(8,128)} reshape(f32[384,8,96]{2,1,0:T(8,128)} %copy.83) | data formatting | bytes 2359296 | tf_op jit(solution)/shard_map/concatenate | solution.py:97
  183.5 3.0 %copy.82 = f32[384,8,96]{2,1,0:T(8,128)} copy(f32[384,8,96]{0,2,1:T(8,128)} %fusion.13) | data formatting | bytes 2359296 | tf_op jit(solution)/shard_map/mul | solution.py:94
  186.5 2.7 concatenate.35
  189.1 1.5 constant_dynamic-update-slice_fusion.1
  191.0 1.5 copy-done.6
  193.4 1.9 collective-permute-start.4
  195.3 7.5 %collective-permute-start.5 = (f32[8,8,1536]{2,1,0:T(8,128)}, f32[8,8,1536]{2,1,0:T(8,128)}, u32[]{:S(2)}, u32[]{:S(2)}) collective-permute-start(f32[8,8,1536]{2,1,0:T(8,128)} %get-tuple-element.10), channel_id=1, source_target_pairs={{0,15},{1,0},{2,1},{3,2},{4,3},{5,4},{6,5},{7,6},{8,7},{9,8},{10,9... | collective-permute-start | bytes 1179656 | tf_op jit(solution)/shard_map/ppermute | solution.py:33
  204.0 1.4 fusion.19
  206.4 4.2 %all-to-all-start = ((bf16[16,8,6,320]{3,1,2,0:T(8,128)(2,1)}), bf16[16,8,6,320]{3,1,2,0:T(8,128)(2,1)}, u32[]{:S(2)}, u32[]{:S(2)}) async-start(bf16[16,8,6,320]{3,1,2,0:T(8,128)(2,1)} %bitcast.121), calls=%async_computation | async-start | bytes 1179648 | tf_op jit(solution)/shard_map/all_to_all | solution.py:159
  212.0 2.0 fusion.10
  214.0 9.3 %all-to-all-done = bf16[16,8,6,320]{3,1,2,0:T(8,128)(2,1)} async-done(((bf16[16,8,6,320]{3,1,2,0:T(8,128)(2,1)}), bf16[16,8,6,320]{3,1,2,0:T(8,128)(2,1)}, u32[]{:S(2)}, u32[]{:S(2)}) %all-to-all-start) | async-done | bytes 491552 | tf_op jit(solution)/shard_map/all_to_all | solution.py:159
  225.2 7.7 %all-to-all-start.1 = ((f32[16,6,320]{2,1,0:T(8,128)}), f32[16,6,320]{2,1,0:T(8,128)S(1)}, u32[]{:S(2)}, u32[]{:S(2)}) async-start(f32[16,6,320]{2,1,0:T(8,128)} %bitcast.39), calls=%async_computation.1 | async-start | bytes 393216 | tf_op jit(solution)/shard_map/all_to_all | solution.py:162
  232.9 6.8 %fusion.63 = (f32[256]{0:T(256)S(1)}, f32[256]{0:T(256)S(1)}, f32[256,1536]{1,0:T(8,128)}) fusion(f32[256]{0:T(256)S(1)} %rsqrt.12, f32[256]{0:T(256)S(1)} %div.51, bf16[1,8,32,1536]{3,2,1,0:T(8,128)(2,1)S(1)} %copy-done.2, f32[1536]{0:T(1024)S(1)} %copy-done.24, bf16[1536,1152]{1,0:T(8,128)(2,1)} %copy-done.11, bf16[1536,1152]{1,0:T(8,128)(2,1)} %copy-done.10, ...), kind=kOutput, calls=%fused_computation.128 | convolution fusion | flops 1831206400 | bytes 10627072 | tf_op jit(solution)/shard_map/dot_general | solution.py:121
  239.7 8.8 %all-to-all-done.1 = f32[16,6,320]{2,1,0:T(8,128)S(1)} async-done(((f32[16,6,320]{2,1,0:T(8,128)}), f32[16,6,320]{2,1,0:T(8,128)S(1)}, u32[]{:S(2)}, u32[]{:S(2)}) %all-to-all-start.1) | async-done | bytes 122912 | tf_op jit(solution)/shard_map/all_to_all | solution.py:162
  249.2 3.5 %all-to-all-start.2 = ((f32[16,6,320]{2,1,0:T(8,128)}), f32[16,6,320]{2,1,0:T(8,128)S(1)}, u32[]{:S(2)}, u32[]{:S(2)}) async-start(f32[16,6,320]{2,1,0:T(8,128)} %broadcast_in_dim.80), calls=%async_computation.2 | async-start | bytes 393216 | tf_op jit(solution)/shard_map/all_to_all | solution.py:165
  252.8 2.9 %add_convert_fusion = bf16[256,1536]{1,0:T(8,128)(2,1)} fusion(f32[256,1536]{1,0:T(8,128)S(1)} %copy-done.4, f32[256,1536]{1,0:T(8,128)} %get-tuple-element.23, bf16[1,8,32,1536]{3,2,1,0:T(8,128)(2,1)S(1)} %copy-done.2, f32[256]{0:T(256)S(1)} %get-tuple-element.32, f32[256]{0:T(256)S(1)} %get-tuple-element.33, f32[256]{0:T(256)S(1)} %rsqrt.12, f32[256]{0:T(256)S(1)} %div.51), kind=kLoop, calls=%fused_computation.21 | loop fusion | flops 3538944 | bytes 4722688 | tf_op jit(solution)/shard_map/convert_element_type | solution.py:236
  255.7 5.4 %all-to-all-done.2 = f32[16,6,320]{2,1,0:T(8,128)S(1)} async-done(((f32[16,6,320]{2,1,0:T(8,128)}), f32[16,6,320]{2,1,0:T(8,128)S(1)}, u32[]{:S(2)}, u32[]{:S(2)}) %all-to-all-start.2) | async-done | bytes 122912 | tf_op jit(solution)/shard_map/all_to_all | solution.py:165
  (108 shorter events, 28.8 us)
Async XLA Ops:
  7.2 1.9 copy-start
  7.2 2.7 %copy-start.18 = (f32[1,20,8,32]{3,2,1,0:T(8,128)S(1)}, f32[1,20,8,32]{3,2,1,0:T(8,128)}, u32[]{:S(2)}) copy-start(f32[1,20,8,32]{3,2,1,0:T(8,128)} %param.12) | copy-start | bytes 61444
  7.2 12.0 %copy-start.22 = (f32[1,20,32,128]{3,2,1,0:T(8,128)S(1)}, f32[1,20,32,128]{3,2,1,0:T(8,128)}, u32[]{:S(2)}) copy-start(f32[1,20,32,128]{3,2,1,0:T(8,128)} %param.13) | copy-start | bytes 983044
  7.2 90.1 %all-gather.2.cloned.1.call-start = ((), (), s32[]{:S(2)}) async-start(), calls=%async_computation.3 | async-start | bytes 11354112 | tf_op jit(solution)/shard_map/all_gather | solution.py:143
  10.0 15.7 %collective-permute-start.2 = (f32[20,8,1]{2,1,0:T(8,128)S(1)}, f32[20,8,1]{2,1,0:T(8,128)S(1)}, u32[]{:S(2)}, u32[]{:S(2)}) collective-permute-start(f32[20,8,1]{2,1,0:T(8,128)S(1)} %get-tuple-element.17), channel_id=1, source_target_pairs={{0,1},{1,2},{2,3},{3,4},{4,5},{5,6},{6,7},{7,8},{8,9},{9,10},{10,1... | collective-permute-start | bytes 1928 | tf_op jit(solution)/shard_map/ppermute | solution.py:24
  13.4 12.3 %collective-permute-start.3 = (f32[20,8,1]{2,1,0:T(8,128)S(1)}, f32[20,8,1]{2,1,0:T(8,128)S(1)}, u32[]{:S(2)}, u32[]{:S(2)}) collective-permute-start(f32[20,8,1]{2,1,0:T(8,128)S(1)} %get-tuple-element.18), channel_id=1, source_target_pairs={{1,0},{2,1},{3,2},{4,3},{5,4},{6,5},{7,6},{8,7},{9,8},{10,9},{11,1... | collective-permute-start | bytes 1928 | tf_op jit(solution)/shard_map/ppermute | solution.py:25
  19.8 3.7 %copy-start.2 = (bf16[1,8,32,1536]{3,2,1,0:T(8,128)(2,1)S(1)}, bf16[1,8,32,1536]{3,2,1,0:T(8,128)(2,1)}, u32[]{:S(2)}) copy-start(bf16[1,8,32,1536]{3,2,1,0:T(8,128)(2,1)} %param.7) | copy-start | bytes 2359300
  21.3 4.2 %copy-start.23 = (f32[1536]{0:T(1024)S(1)}, f32[1536]{0:T(1024)}, u32[]{:S(2)}) copy-start(f32[1536]{0:T(1024)} %param.8) | copy-start | bytes 18436
  105.6 3.8 %copy-start.10 = (bf16[1536,1152]{1,0:T(8,128)(2,1)}, bf16[1536,1152]{1,0:T(8,128)(2,1)S(1)}, u32[]{:S(2)}) copy-start(bf16[1536,1152]{1,0:T(8,128)(2,1)S(1)} %get-tuple-element.7) | copy-start | bytes 10616836
  105.6 3.8 %copy-start.11 = (bf16[1536,1152]{1,0:T(8,128)(2,1)}, bf16[1536,1152]{1,0:T(8,128)(2,1)S(1)}, u32[]{:S(2)}) copy-start(bf16[1536,1152]{1,0:T(8,128)(2,1)S(1)} %get-tuple-element.8) | copy-start | bytes 10616836
  123.1 16.1 %collective-permute-start = (bf16[8,8,1536]{2,1,0:T(8,128)(2,1)}, bf16[8,8,1536]{2,1,0:T(8,128)(2,1)}, u32[]{:S(2)}, u32[]{:S(2)}) collective-permute-start(bf16[8,8,1536]{2,1,0:T(8,128)(2,1)} %get-tuple-element.13), channel_id=1, source_target_pairs={{0,1},{1,2},{2,3},{3,4},{4,5},{5,6},{6,7},{7,8},{8,9},{9,10},{10,1... | collective-permute-start | bytes 589832 | tf_op jit(solution)/shard_map/ppermute | solution.py:24
  126.4 12.7 %collective-permute-start.1 = (bf16[8,8,1536]{2,1,0:T(8,128)(2,1)}, bf16[8,8,1536]{2,1,0:T(8,128)(2,1)}, u32[]{:S(2)}, u32[]{:S(2)}) collective-permute-start(bf16[8,8,1536]{2,1,0:T(8,128)(2,1)} %get-tuple-element.14), channel_id=1, source_target_pairs={{1,0},{2,1},{3,2},{4,3},{5,4},{6,5},{7,6},{8,7},{9,8},{10,9},{11,1... | collective-permute-start | bytes 589832 | tf_op jit(solution)/shard_map/ppermute | solution.py:25
  134.5 1.1 copy-start.3
  149.8 3.0 %copy-start.5 = (f32[8,256,384]{2,1,0:T(8,128)S(1)}, f32[8,256,384]{2,1,0:T(8,128)}, u32[]{:S(2)}) copy-start(f32[8,256,384]{2,1,0:T(8,128)} %get-tuple-element.20) | copy-start | bytes 9437188
  149.8 3.1 %copy-start.21 = (bf16[256,768]{0,1:T(8,128)(2,1)S(1)}, bf16[256,768]{0,1:T(8,128)(2,1)}, u32[]{:S(2)}) copy-start(bf16[256,768]{0,1:T(8,128)(2,1)} %copy.81) | copy-start | bytes 1179652
  152.9 1.6 copy-start.20
  155.5 1.1 copy-start.8
  161.1 2.4 copy-start.19
  165.1 3.1 %copy-start.12 = (bf16[1536,160]{1,0:T(8,128)(2,1)S(1)}, bf16[1536,160]{1,0:T(8,128)(2,1)}, u32[]{:S(2)}) copy-start(bf16[1536,160]{1,0:T(8,128)(2,1)} %get-tuple-element.5) | copy-start | bytes 1474564
  165.2 3.1 %copy-start.13 = (bf16[1536,160]{1,0:T(8,128)(2,1)S(1)}, bf16[1536,160]{1,0:T(8,128)(2,1)}, u32[]{:S(2)}) copy-start(bf16[1536,160]{1,0:T(8,128)(2,1)} %get-tuple-element.6) | copy-start | bytes 1474564
  165.2 3.1 %copy-start.14 = (bf16[256,1536]{1,0:T(8,128)(2,1)S(1)}, bf16[256,1536]{1,0:T(8,128)(2,1)}, u32[]{:S(2)}) copy-start(bf16[256,1536]{1,0:T(8,128)(2,1)} %fusion.8) | copy-start | bytes 2359300
  166.3 37.7 %collective-permute-start.6 = (f32[8,96,320]{2,1,0:T(8,128)}, f32[8,96,320]{2,1,0:T(8,128)}, u32[]{:S(2)}, u32[]{:S(2)}) collective-permute-start(f32[8,96,320]{2,1,0:T(8,128)} %dynamic-slice_bitcast_fusion), channel_id=1, source_target_pairs={{0,16},{16,0},{1,17},{17,1},{2,18},{18,2},{3,19},{19,3},{4,20},{20... | collective-permute-start | bytes 2949128 | tf_op jit(solution)/shard_map/ppermute | solution.py:157
  179.7 2.8 %copy-start.15 = (bf16[8,96,256]{2,1,0:T(8,128)(2,1)S(1)}, bf16[8,96,256]{2,1,0:T(8,128)(2,1)}, u32[]{:S(2)}) copy-start(bf16[8,96,256]{2,1,0:T(8,128)(2,1)} %fusion.14) | copy-start | bytes 1179652
  189.1 1.6 copy-start.9
  190.8 12.0 %copy-start.16 = (f32[20,32,128]{2,1,0:T(8,128)S(1)}, f32[20,32,128]{2,1,0:T(8,128)}, u32[]{:S(2)}) copy-start(f32[20,32,128]{2,1,0:T(8,128)} %copy.78) | copy-start | bytes 983044
  190.8 12.0 %copy-start.17 = (f32[20,32,34]{2,1,0:T(8,128)S(1)}, f32[20,32,34]{2,1,0:T(8,128)}, u32[]{:S(2)}) copy-start(f32[20,32,34]{2,1,0:T(8,128)} %convolution_bitcast_fusion.2) | copy-start | bytes 261124
  190.8 12.0 %copy-start.25 = (s32[128]{0:T(128)S(1)}, s32[128]{0:T(128)}, u32[]{:S(2)}) copy-start(s32[128]{0:T(128)} %get-tuple-element.30) | copy-start | bytes 1540
  190.8 12.0 %copy-start.26 = (s32[128]{0:T(128)S(1)}, s32[128]{0:T(128)}, u32[]{:S(2)}) copy-start(s32[128]{0:T(128)} %get-tuple-element.31) | copy-start | bytes 1540
  190.8 12.1 %copy-start.27 = (f32[128]{0:T(128)S(1)}, f32[128]{0:T(128)}, u32[]{:S(2)}) copy-start(f32[128]{0:T(128)} %get-tuple-element.24) | copy-start | bytes 1540
  190.8 12.0 %copy-start.28 = (f32[128]{0:T(128)S(1)}, f32[128]{0:T(128)}, u32[]{:S(2)}) copy-start(f32[128]{0:T(128)} %get-tuple-element.25) | copy-start | bytes 1540
  191.0 1.5 copy-start.6
  193.4 17.3 %collective-permute-start.4 = (f32[8,8,1536]{2,1,0:T(8,128)}, f32[8,8,1536]{2,1,0:T(8,128)S(1)}, u32[]{:S(2)}, u32[]{:S(2)}) collective-permute-start(f32[8,8,1536]{2,1,0:T(8,128)} %get-tuple-element.9), channel_id=1, source_target_pairs={{0,1},{1,2},{2,3},{3,4},{4,5},{5,6},{6,7},{7,8},{8,9},{9,10},{10,1... | collective-permute-start | bytes 1179656 | tf_op jit(solution)/shard_map/ppermute | solution.py:33
  195.3 16.7 %collective-permute-start.5 = (f32[8,8,1536]{2,1,0:T(8,128)}, f32[8,8,1536]{2,1,0:T(8,128)}, u32[]{:S(2)}, u32[]{:S(2)}) collective-permute-start(f32[8,8,1536]{2,1,0:T(8,128)} %get-tuple-element.10), channel_id=1, source_target_pairs={{0,15},{1,0},{2,1},{3,2},{4,3},{5,4},{6,5},{7,6},{8,7},{9,8},{10,9... | collective-permute-start | bytes 1179656 | tf_op jit(solution)/shard_map/ppermute | solution.py:33
  205.4 6.6 %copy-start.7 = (f32[8,48,1536]{2,1,0:T(8,128)S(1)}, f32[8,48,1536]{2,1,0:T(8,128)}, u32[]{:S(2)}) copy-start(f32[8,48,1536]{2,1,0:T(8,128)} %copy-done.6) | copy-start | bytes 7077892
  206.4 16.9 %all-to-all-start = ((bf16[16,8,6,320]{3,1,2,0:T(8,128)(2,1)}), bf16[16,8,6,320]{3,1,2,0:T(8,128)(2,1)}, u32[]{:S(2)}, u32[]{:S(2)}) async-start(bf16[16,8,6,320]{3,1,2,0:T(8,128)(2,1)} %bitcast.121), calls=%async_computation | async-start | bytes 1179648 | tf_op jit(solution)/shard_map/all_to_all | solution.py:159
  210.7 22.2 %copy-start.24 = (f32[1536]{0:T(1024)S(1)}, f32[1536]{0:T(1024)}, u32[]{:S(2)}) copy-start(f32[1536]{0:T(1024)} %param.8) | copy-start | bytes 18436
  225.2 23.3 %all-to-all-start.1 = ((f32[16,6,320]{2,1,0:T(8,128)}), f32[16,6,320]{2,1,0:T(8,128)S(1)}, u32[]{:S(2)}, u32[]{:S(2)}) async-start(f32[16,6,320]{2,1,0:T(8,128)} %bitcast.39), calls=%async_computation.1 | async-start | bytes 393216 | tf_op jit(solution)/shard_map/all_to_all | solution.py:162
  232.9 19.9 %copy-start.4 = (f32[256,1536]{1,0:T(8,128)S(1)}, f32[256,1536]{1,0:T(8,128)}, u32[]{:S(2)}) copy-start(f32[256,1536]{1,0:T(8,128)} %copy-done.3) | copy-start | bytes 4718596
  249.2 11.8 %all-to-all-start.2 = ((f32[16,6,320]{2,1,0:T(8,128)}), f32[16,6,320]{2,1,0:T(8,128)S(1)}, u32[]{:S(2)}, u32[]{:S(2)}) async-start(f32[16,6,320]{2,1,0:T(8,128)} %broadcast_in_dim.80), calls=%async_computation.2 | async-start | bytes 393216 | tf_op jit(solution)/shard_map/all_to_all | solution.py:165
  252.8 9.0 %copy-start.1 = (bf16[96,2304]{1,0:T(8,128)(2,1)S(1)}, bf16[96,2304]{1,0:T(8,128)(2,1)}, u32[]{:S(2)}) copy-start(bf16[96,2304]{1,0:T(8,128)(2,1)} %param.9) | copy-start | bytes 1327108
Sparse Core Ops, SparseCore 0:
  10.7 86.5 all-gather.1
where the time goes:
time: 270 us; the launch traced here: 269 us
  waiting for transfers between devices  95.1 us (35%)
  local copies, waits for them, and re-layouts  67.9 us (25%)
  starting transfers between devices  45.3 us (17%)
  matrix products  33.3 us (12%)
  between operations  14.6 us (5%)
  other arithmetic  12.4 us (5%)
    all_gather x1, waiting for transfers between devices, gather_weights(): full = lax.all_gather(packed, ('dp',) + FSDP, axis=0, tiled=True)  70.3 us
    ppermute x2, starting transfers between devices, with_halo(): after = lax.ppermute(leading, axis, down)  11.7 us
    dot_general x3, matrix products, contract_last(): lax.dot_general(left_side, right_side, (((1,), (1,)), ((), ())), preferre...  10.5 us
    ppermute x2, starting transfers between devices, from_behind(): return lax.ppermute(value, axis, pairs)  9.37 us
    all_to_all x1, waiting for transfers between devices, reduce_head(): pieces = lax.all_to_all(pieces, TILE, 0, 0, tiled=True)  9.29 us
    unnamed x61, local copies, waits for them, and re-layouts  9.08 us
    all_to_all x1, waiting for transfers between devices, reduce_head(): both = lax.all_to_all(both, ('dp', 'z'), 0, 0, tiled=True)  8.76 us
    all_to_all x1, starting transfers between devices, reduce_head(): both = lax.all_to_all(both, ('dp', 'z'), 0, 0, tiled=True)  7.69 us
  transfers between devices with their start and end apart: 11, of which 5 were waited for; matrix products, arithmetic and copies ran while one was open for 19% of the time, Pallas kernels for 0%

commit v1 on v0

--- a/solution.py
+++ b/solution.py
@@ -140,7 +140,10 @@
     out_half = jnp.concatenate([out_half[:, :384], out_half[:, 384:]], axis=0)
     head_half = lax.dynamic_slice_in_dim(head_w, half * 160, 160, 1)
     packed = jnp.concatenate([qkv_half, out_half, head_half], axis=1)
-    full = lax.all_gather(packed, ("dp",) + FSDP, axis=0, tiled=True)
+    full = jnp.concatenate(
+        lax.all_to_all(jnp.stack([packed] * lax.axis_size(("dp",) + FSDP)), ("dp",) + FSDP, 0, 0),
+        axis=0,
+    )
     full = full.reshape(2, D, 1696)
     full_qkv = jnp.concatenate([full[0, :, :HALF_QKV], full[1, :, :HALF_QKV]], axis=1)
     out_part = full[:, :, HALF_QKV:1536].reshape(2, 16, 2, 48, 384)

time: 270 us -> 659 us (2.44)
  waiting for transfers between devices: 95.1 us -> 491 us
  between operations: 14.6 us -> 1.2 us
  starting transfers between devices: 45.3 us -> 57.3 us
    all_to_all x0 -> x1, waiting for transfers between devices: none -> 466 us  [gather_weights(): lax.all_to_all(jnp.stack([packed] * lax.axis_size(('dp',) + FSDP)), ('dp'...]
    all_gather x1 -> x0, waiting for transfers between devices: 70.3 us -> none  [gather_weights(): full = lax.all_gather(packed, ('dp',) + FSDP, axis=0, tiled=True)]
    all_to_all x0 -> x1, starting transfers between devices: none -> 15.4 us  [gather_weights(): lax.all_to_all(jnp.stack([packed] * lax.axis_size(('dp',) + FSDP)), ('dp'...]
  transfers between devices with their start and end apart: 11 -> 11, of which waited for: 5 -> 6; matrix products, arithmetic and copies ran while one was open for 19% -> 7% of each run, Pallas kernels for 0% -> 0%
where the time goes in v1:
time: 659 us; the launch traced here: 658 us
  waiting for transfers between devices  491 us (75%)
  local copies, waits for them, and re-layouts  67.3 us (10%)
  starting transfers between devices  57.3 us (9%)
  matrix products  31.4 us (5%)
  other arithmetic  9.95 us (2%)
    all_to_all x1, waiting for transfers between devices, gather_weights(): lax.all_to_all(jnp.stack([packed] * lax.axis_size(('dp',) + FSDP)), ('dp'...  466 us
    all_to_all x1, starting transfers between devices, gather_weights(): lax.all_to_all(jnp.stack([packed] * lax.axis_size(('dp',) + FSDP)), ('dp'...  15.4 us
  transfers between devices with their start and end apart: 11, of which 6 were waited for; matrix products, arithmetic and copies ran while one was open for 7% of the time, Pallas kernels for 0%

profile of v1, /device:TPU:32, one launch (start us, length us, event | category | flops | bytes accessed | tf_op | source)
XLA Modules:
  0.0 657.8 jit_solution(6848611531822275728)
XLA Ops:
  2.6 5.3 stack.2
  7.9 15.4 %all-to-all-start = ((bf16[32,96,1696]{2,1,0:T(8,128)(2,1)}), bf16[32,96,1696]{2,1,0:T(8,128)(2,1)}, u32[]{:S(2)}, u32[]{:S(2)}) async-start(bf16[32,96,1696]{2,1,0:T(8,128)(2,1)} %stack.2), calls=%async_computation | async-start | bytes 22020096 | tf_op jit(solution)/shard_map/all_to_all | solution.py:144
  23.4 3.4 collective-permute-start.2
  26.8 5.8 collective-permute-start.3
  33.2 1.5 copy.80
  37.9 466.3 %all-to-all-done = bf16[32,96,1696]{2,1,0:T(8,128)(2,1)} async-done(((bf16[32,96,1696]{2,1,0:T(8,128)(2,1)}), bf16[32,96,1696]{2,1,0:T(8,128)(2,1)}, u32[]{:S(2)}, u32[]{:S(2)}) %all-to-all-start) | async-done | bytes 10420256 | tf_op jit(solution)/shard_map/all_to_all | solution.py:144
  504.3 2.7 slice_bitcast_fusion.3
  506.9 1.9 slice.82
  508.8 3.6 slice_bitcast_fusion.1
  512.5 3.8 fusion.3
  517.2 3.7 copy.76
  520.9 5.3 reshape.210
  526.4 1.8 fusion.66
  528.2 3.4 collective-permute-start
  531.6 5.9 collective-permute-start.1
  537.5 2.1 convolution_bitcast_fusion
  546.4 2.1 copy.91
  548.5 2.9 fusion.68
  551.4 2.9 convolution_convert_fusion.1
  554.4 1.6 convolution_bitcast_fusion.1
  557.8 1.4 fusion.14
  559.2 1.4 fusion.13
  560.6 1.7 fusion.8
  562.3 2.4 copy.85
  564.7 1.7 fusion.26
  567.5 1.9 collective-permute-start.6
  570.5 1.4 reshape.211
  571.9 3.1 copy.77
  575.0 2.3 copy.78
  577.2 3.0 copy.83
  580.2 2.8 concatenate.36
  584.0 3.0 copy.82
  587.0 2.7 concatenate.35
  589.7 1.5 constant_dynamic-update-slice_fusion.1
  591.5 1.5 copy-done.8
  593.9 1.9 collective-permute-start.4
  595.8 7.5 %collective-permute-start.5 = (f32[8,8,1536]{2,1,0:T(8,128)}, f32[8,8,1536]{2,1,0:T(8,128)}, u32[]{:S(2)}, u32[]{:S(2)}) collective-permute-start(f32[8,8,1536]{2,1,0:T(8,128)} %get-tuple-element.10), channel_id=1, source_target_pairs={{0,15},{1,0},{2,1},{3,2},{4,3},{5,4},{6,5},{7,6},{8,7},{9,8},{10,9... | collective-permute-start | bytes 1179656 | tf_op jit(solution)/shard_map/ppermute | solution.py:33
  604.5 1.4 fusion.19
  606.9 3.6 all-to-all-start.1
  610.9 3.7 collective-permute-done.5
  614.6 2.5 fusion.10
  617.0 6.0 all-to-all-done.1
  623.9 5.0 all-to-all-start.2
  628.9 6.8 %fusion.63 = (f32[256]{0:T(256)S(1)}, f32[256]{0:T(256)S(1)}, f32[256,1536]{1,0:T(8,128)}) fusion(f32[256]{0:T(256)S(1)} %rsqrt.12, f32[256]{0:T(256)S(1)} %div.51, bf16[1,8,32,1536]{3,2,1,0:T(8,128)(2,1)S(1)} %copy-done.4, f32[1536]{0:T(1024)S(1)} %copy-done.23, bf16[1536,1152]{1,0:T(8,128)(2,1)} %copy-done.11, bf16[1536,1152]{1,0:T(8,128)(2,1)} %copy-done.10, ...), kind=kOutput, calls=%fused_computation.128 | convolution fusion | flops 1831206400 | bytes 10627072 | tf_op jit(solution)/shard_map/dot_general | solution.py:121
  635.8 8.7 %all-to-all-done.2 = f32[16,6,320]{2,1,0:T(8,128)S(1)} async-done(((f32[16,6,320]{2,1,0:T(8,128)}), f32[16,6,320]{2,1,0:T(8,128)S(1)}, u32[]{:S(2)}, u32[]{:S(2)}) %all-to-all-start.2) | async-done | bytes 122912 | tf_op jit(solution)/shard_map/all_to_all | solution.py:165
  645.2 3.5 all-to-all-start.3
  648.8 2.9 add_convert_fusion
  651.7 5.4 all-to-all-done.3
  (98 shorter events, 24.5 us)
Async XLA Ops:
  0.6 1.9 copy-start
  7.9 15.5 %copy-start.17 = (f32[1,20,8,32]{3,2,1,0:T(8,128)S(1)}, f32[1,20,8,32]{3,2,1,0:T(8,128)}, u32[]{:S(2)}) copy-start(f32[1,20,8,32]{3,2,1,0:T(8,128)} %param.12) | copy-start | bytes 61444
  7.9 24.7 %copy-start.20 = (f32[1,20,32,128]{3,2,1,0:T(8,128)S(1)}, f32[1,20,32,128]{3,2,1,0:T(8,128)}, u32[]{:S(2)}) copy-start(f32[1,20,32,128]{3,2,1,0:T(8,128)} %param.13) | copy-start | bytes 983044
  7.9 496.4 %all-to-all-start = ((bf16[32,96,1696]{2,1,0:T(8,128)(2,1)}), bf16[32,96,1696]{2,1,0:T(8,128)(2,1)}, u32[]{:S(2)}, u32[]{:S(2)}) async-start(bf16[32,96,1696]{2,1,0:T(8,128)(2,1)} %stack.2), calls=%async_computation | async-start | bytes 22020096 | tf_op jit(solution)/shard_map/all_to_all | solution.py:144
  23.4 13.2 %collective-permute-start.2 = (f32[20,8,1]{2,1,0:T(8,128)S(1)}, f32[20,8,1]{2,1,0:T(8,128)S(1)}, u32[]{:S(2)}, u32[]{:S(2)}) collective-permute-start(f32[20,8,1]{2,1,0:T(8,128)S(1)} %get-tuple-element.17), channel_id=1, source_target_pairs={{0,1},{1,2},{2,3},{3,4},{4,5},{5,6},{6,7},{7,8},{8,9},{9,10},{10,1... | collective-permute-start | bytes 1928 | tf_op jit(solution)/shard_map/ppermute | solution.py:24
  26.8 9.9 %collective-permute-start.3 = (f32[20,8,1]{2,1,0:T(8,128)S(1)}, f32[20,8,1]{2,1,0:T(8,128)S(1)}, u32[]{:S(2)}, u32[]{:S(2)}) collective-permute-start(f32[20,8,1]{2,1,0:T(8,128)S(1)} %get-tuple-element.18), channel_id=1, source_target_pairs={{1,0},{2,1},{3,2},{4,3},{5,4},{6,5},{7,6},{8,7},{9,8},{10,9},{11,1... | collective-permute-start | bytes 1928 | tf_op jit(solution)/shard_map/ppermute | solution.py:25
  33.2 2.4 copy-start.2
  34.7 1.7 copy-start.23
  35.9 593.0 %copy-start.21 = (f32[256]{0:T(256)}, f32[256]{0:T(256)S(1)}, u32[]{:S(2)}) copy-start(f32[256]{0:T(256)S(1)} %div.51) | copy-start | bytes 3076
  36.3 592.6 %copy-start.22 = (f32[256]{0:T(256)}, f32[256]{0:T(256)S(1)}, u32[]{:S(2)}) copy-start(f32[256]{0:T(256)S(1)} %rsqrt.12) | copy-start | bytes 3076
  512.4 3.8 copy-start.10
  512.5 3.8 copy-start.11
  528.2 14.4 %collective-permute-start = (bf16[8,8,1536]{2,1,0:T(8,128)(2,1)}, bf16[8,8,1536]{2,1,0:T(8,128)(2,1)}, u32[]{:S(2)}, u32[]{:S(2)}) collective-permute-start(bf16[8,8,1536]{2,1,0:T(8,128)(2,1)} %get-tuple-element.13), channel_id=1, source_target_pairs={{0,1},{1,2},{2,3},{3,4},{4,5},{5,6},{6,7},{7,8},{8,9},{9,10},{10,1... | collective-permute-start | bytes 589832 | tf_op jit(solution)/shard_map/ppermute | solution.py:24
  531.6 11.0 %collective-permute-start.1 = (bf16[8,8,1536]{2,1,0:T(8,128)(2,1)}, bf16[8,8,1536]{2,1,0:T(8,128)(2,1)}, u32[]{:S(2)}, u32[]{:S(2)}) collective-permute-start(bf16[8,8,1536]{2,1,0:T(8,128)(2,1)} %get-tuple-element.14), channel_id=1, source_target_pairs={{1,0},{2,1},{3,2},{4,3},{5,4},{6,5},{7,6},{8,7},{9,8},{10,9},{11,1... | collective-permute-start | bytes 589832 | tf_op jit(solution)/shard_map/ppermute | solution.py:25
  539.6 1.2 copy-start.5
  551.4 3.0 copy-start.7
  551.4 3.1 copy-start.19
  554.4 1.6 copy-start.18
  559.2 1.4 copy-start.3
  566.4 3.1 copy-start.12
  566.4 3.1 copy-start.13
  566.4 3.1 copy-start.14
  567.5 36.9 %collective-permute-start.6 = (f32[8,96,320]{2,1,0:T(8,128)}, f32[8,96,320]{2,1,0:T(8,128)}, u32[]{:S(2)}, u32[]{:S(2)}) collective-permute-start(f32[8,96,320]{2,1,0:T(8,128)} %dynamic-slice_bitcast_fusion), channel_id=1, source_target_pairs={{0,16},{16,0},{1,17},{17,1},{2,18},{18,2},{3,19},{19,3},{4,20},{20... | collective-permute-start | bytes 2949128 | tf_op jit(solution)/shard_map/ppermute | solution.py:160
  580.2 2.8 copy-start.15
  589.7 1.6 copy-start.9
  591.3 12.0 %copy-start.16 = (f32[20,32,34]{2,1,0:T(8,128)S(1)}, f32[20,32,34]{2,1,0:T(8,128)}, u32[]{:S(2)}) copy-start(f32[20,32,34]{2,1,0:T(8,128)} %convolution_bitcast_fusion.2) | copy-start | bytes 261124
  591.5 1.5 copy-start.8
  593.9 16.9 %collective-permute-start.4 = (f32[8,8,1536]{2,1,0:T(8,128)}, f32[8,8,1536]{2,1,0:T(8,128)S(1)}, u32[]{:S(2)}, u32[]{:S(2)}) collective-permute-start(f32[8,8,1536]{2,1,0:T(8,128)} %get-tuple-element.9), channel_id=1, source_target_pairs={{0,1},{1,2},{2,3},{3,4},{4,5},{5,6},{6,7},{7,8},{8,9},{9,10},{10,1... | collective-permute-start | bytes 1179656 | tf_op jit(solution)/shard_map/ppermute | solution.py:33
  595.8 18.7 %collective-permute-start.5 = (f32[8,8,1536]{2,1,0:T(8,128)}, f32[8,8,1536]{2,1,0:T(8,128)}, u32[]{:S(2)}, u32[]{:S(2)}) collective-permute-start(f32[8,8,1536]{2,1,0:T(8,128)} %get-tuple-element.10), channel_id=1, source_target_pairs={{0,15},{1,0},{2,1},{3,2},{4,3},{5,4},{6,5},{7,6},{8,7},{9,8},{10,9... | collective-permute-start | bytes 1179656 | tf_op jit(solution)/shard_map/ppermute | solution.py:33
  606.9 16.2 %all-to-all-start.1 = ((bf16[16,8,6,320]{3,1,2,0:T(8,128)(2,1)}), bf16[16,8,6,320]{3,1,2,0:T(8,128)(2,1)S(1)}, u32[]{:S(2)}, u32[]{:S(2)}) async-start(bf16[16,8,6,320]{3,1,2,0:T(8,128)(2,1)} %bitcast.38), calls=%async_computation.1 | async-start | bytes 1179648 | tf_op jit(solution)/shard_map/all_to_all | solution.py:162
  610.5 18.4 %copy-start.4 = (bf16[1,8,32,1536]{3,2,1,0:T(8,128)(2,1)S(1)}, bf16[1,8,32,1536]{3,2,1,0:T(8,128)(2,1)}, u32[]{:S(2)}) copy-start(bf16[1,8,32,1536]{3,2,1,0:T(8,128)(2,1)} %param.7) | copy-start | bytes 2359300
  623.9 20.6 %all-to-all-start.2 = ((f32[16,6,320]{2,1,0:T(8,128)}), f32[16,6,320]{2,1,0:T(8,128)S(1)}, u32[]{:S(2)}, u32[]{:S(2)}) async-start(f32[16,6,320]{2,1,0:T(8,128)} %bitcast.39), calls=%async_computation.2 | async-start | bytes 393216 | tf_op jit(solution)/shard_map/all_to_all | solution.py:165
  628.9 19.9 %copy-start.6 = (f32[256,1536]{1,0:T(8,128)S(1)}, f32[256,1536]{1,0:T(8,128)}, u32[]{:S(2)}) copy-start(f32[256,1536]{1,0:T(8,128)} %copy-done.5) | copy-start | bytes 4718596
  645.2 11.8 %all-to-all-start.3 = ((f32[16,6,320]{2,1,0:T(8,128)}), f32[16,6,320]{2,1,0:T(8,128)S(1)}, u32[]{:S(2)}, u32[]{:S(2)}) async-start(f32[16,6,320]{2,1,0:T(8,128)} %broadcast_in_dim.80), calls=%async_computation.3 | async-start | bytes 393216 | tf_op jit(solution)/shard_map/all_to_all | solution.py:168
  648.8 9.0 %copy-start.1 = (bf16[96,2304]{1,0:T(8,128)(2,1)S(1)}, bf16[96,2304]{1,0:T(8,128)(2,1)}, u32[]{:S(2)}) copy-start(bf16[96,2304]{1,0:T(8,128)(2,1)} %param.9) | copy-start | bytes 1327108
